TPU v7x, 32 devices: a whole 2x2x4 slice. The times are simulated.
32 devices in a mesh: px: 4 (over x, core), py: 8 (over z, y).
Axes of the slice: x: 2, y: 2, z: 4, core: 2. Of those that a mesh axis runs over, the one named last changes fastest.
Arguments:
- fraction: float32 [32, 64, 640], P('px', 'py'), may hold values from 0 to 1
- courant_x: float32 [32, 64, 640], P('px', 'py'), may hold values from -0.5 to 0.5
- courant_y: float32 [32, 64, 640], P('px', 'py'), may hold values from -0.5 to 0.5
- courant_z: float32 [32, 64, 640], P('px', 'py'), may hold values from -0.5 to 0.5
- labels: int32 [32, 64, 640], P('px', 'py'), may hold values from -1 to 31, as said below
- structure_owner: int32 [4, 32], P('px'), may hold values from 0 to 7, as said below
- parcel_owner: int32 [4, 32], P('px'), may hold values from 0 to 7, as said below
Outputs:
- remaining: float32 [32, 64, 640], P('px', 'py')
- moments: float32 [4, 13, 32], P('px', None, 'py')
- parcels: float32 [4, 13, 32], P('px', None, 'py')
Inputs may be any that keep to these rules, and one draw needn't show every extreme that they name: `labels`: a label names a structure of the cell's row. `structure_owner`: in each row every index of py owns exactly 4 structures. `parcel_owner`: in each row every index of py receives exactly 4 parcels.
All inputs are finite; a program needn't handle non-finite values.
Results may differ from a plain program's by a relative error of at most 0.0003.
Values sent between devices are 32-bit elements; how exact they have to be, the bound alone decides.
A program may use at most 64 MiB of HBM per device.

v0:
```python
import math
import jax
import jax.numpy as jnp
from jax import lax
from jax.sharding import PartitionSpec as P


def with_halo(x, sides, width, wrap):
    for axis, dim in sides:
        size, length = (lax.axis_size(axis), x.shape[dim])
        up = [(i, (i + 1) % size) for i in range(size if wrap else size - 1)]
        down = [(j, i) for i, j in up]
        last = lax.slice_in_dim(x, length - width, length, axis=dim)
        initial = lax.slice_in_dim(x, 0, width, axis=dim)
        before = lax.ppermute(last, axis, up)
        after = lax.ppermute(initial, axis, down)
        x = jnp.concatenate([before, x, after], axis=dim)
    return x


def advance(padded_frac, padded_cour, length, axis):

    def part(array, start, count):
        return lax.slice_in_dim(array, start, start + count, axis=axis)

    centre = part(padded_frac, 1, length + 2)
    spread = 0.5 * (part(padded_frac, 2, length + 2) - part(padded_frac, 0, length + 2))
    bound = 2.0 * jnp.minimum(centre, 1.0 - centre)
    slope = jnp.minimum(jnp.maximum(spread, -bound), bound)
    courant = part(padded_cour, 1, length + 1)
    upwind = part(centre, 0, length + 1) + 0.5 * (1.0 - courant) * part(slope, 0, length + 1)
    downwind = part(centre, 1, length + 1) - 0.5 * (1.0 + courant) * part(slope, 1, length + 1)
    flux = courant * jnp.where(courant > 0.0, upwind, downwind)
    middle = part(padded_frac, 2, length)
    high = part(courant, 1, length)
    low = part(courant, 0, length)
    updated = middle - (part(flux, 1, length) - part(flux, 0, length)) + middle * (high - low)
    return (updated, 0.5 * (high + low))


def parcel_rows(moment_rows):
    volume = moment_rows[0]
    safe = jnp.maximum(volume, 0.5)
    centre = moment_rows[1:4] / safe
    velocity = moment_rows[4:7] / safe
    square = moment_rows[7:10] / safe - centre * centre
    cross = jnp.stack(
        [
            moment_rows[10] / safe - centre[0] * centre[1],
            moment_rows[11] / safe - centre[0] * centre[2],
            moment_rows[12] / safe - centre[1] * centre[2],
        ]
    )
    return jnp.concatenate([volume[None], centre, velocity, square, cross], 0)


def slot_table(owner_row, per_owner):
    count = owner_row.shape[0]
    index = jnp.arange(count, dtype=jnp.int32)
    same = owner_row[:, None] == owner_row[None, :]
    earlier = index[None, :] < index[:, None]
    rank = jnp.sum((same & earlier).astype(jnp.int32), axis=1)
    position = owner_row * per_owner + rank
    return (position[:, None] == index[None, :]).astype(jnp.float32)


def product(left, right):
    return jnp.dot(left, right, precision=lax.Precision.HIGHEST, preferred_element_type=jnp.float32)


def local(fraction, courant_x, courant_y, courant_z, labels, structure_owner, parcel_owner):
    rows_x, rows_y, depth = fraction.shape
    padded = with_halo(jnp.stack([fraction, courant_x]), (("px", 1),), 2, True)
    first, velocity_x = advance(padded[0], padded[1], rows_x, 0)
    padded_y = with_halo(jnp.stack([first, courant_y]), (("py", 2),), 2, False)
    second, velocity_y = advance(padded_y[0], padded_y[1], rows_y, 1)
    pad_z = ((0, 0), (0, 0), (2, 2))
    third, velocity_z = advance(jnp.pad(second, pad_z), jnp.pad(courant_z, pad_z), depth, 2)
    remaining = jnp.where(labels >= 0, jnp.float32(0.0), third)
    width_py = lax.axis_size("py")
    row_index = lax.axis_index("py")
    total_x = rows_x * lax.axis_size("px")
    total_y = rows_y * width_py
    structures = structure_owner.shape[1]
    per_owner = structures // width_py
    scale = 4.0 / (rows_x * rows_y * rows_y)
    start_x = lax.axis_index("px") * rows_x
    start_y = row_index * rows_y
    coord_x = ((start_x + jnp.arange(rows_x, dtype=jnp.int32)).astype(jnp.float32) + 0.5)[
        :, None, None
    ] / total_x
    coord_y = ((start_y + jnp.arange(rows_y, dtype=jnp.int32)).astype(jnp.float32) + 0.5)[
        None, :, None
    ] / total_y
    coord_z = (jnp.arange(depth, dtype=jnp.int32).astype(jnp.float32) + 0.5)[None, None, :] / depth
    weight = third * scale
    shape = weight.shape
    cells = rows_x * rows_y * depth
    block = math.gcd(cells, 4096)
    blocks = cells // block
    pieces = [
        jnp.ones(shape, jnp.float32),
        coord_x,
        coord_y,
        coord_z,
        velocity_x,
        velocity_y,
        velocity_z,
        coord_x * coord_x,
        coord_y * coord_y,
        coord_z * coord_z,
        coord_x * coord_y,
        coord_x * coord_z,
        coord_y * coord_z,
    ]
    feature_blocks = jnp.stack(
        [(weight * jnp.broadcast_to(piece, shape)).reshape(blocks, block) for piece in pieces], 1
    )
    label_blocks = labels.reshape(blocks, block)
    columns = jnp.arange(structures, dtype=jnp.int32)

    def accumulate(total, inputs):
        feature_rows, marks = inputs
        onehot = (marks[:, None] == columns[None, :]).astype(jnp.float32)
        return (total + product(feature_rows, onehot), None)

    partial_sums, unused = lax.scan(
        accumulate, jnp.zeros((13, structures), jnp.float32), (feature_blocks, label_blocks)
    )
    owner_slots = slot_table(structure_owner[0], per_owner)
    parcel_slots = slot_table(parcel_owner[0], per_owner)
    mine_owned = lax.dynamic_slice_in_dim(owner_slots, row_index * per_owner, per_owner, 1)
    totals = lax.psum(partial_sums, "py")
    owned = product(totals, mine_owned)
    mine_parcels = lax.dynamic_slice_in_dim(parcel_slots, row_index * per_owner, per_owner, 1)
    received = product(parcel_rows(totals), mine_parcels)
    return (remaining, owned[None], received[None])


def solution(mesh):
    return jax.shard_map(
        local,
        mesh=mesh,
        in_specs=(
            P("px", "py", None),
            P("px", "py", None),
            P("px", "py", None),
            P("px", "py", None),
            P("px", "py", None),
            P("px", None),
            P("px", None),
        ),
        out_specs=(P("px", "py", None), P("px", None, "py"), P("px", None, "py")),
        check_vma=False,
    )
```

profile of v0, /device:TPU:0, one launch (start us, length us, event | category | flops | bytes accessed | tf_op | source)
XLA Modules:
  0.0 86.4 jit_solution(18232538209815463961)
XLA Ops:
  0.7 0.9 %pad_maximum_fusion.7 = (f32[2,2,8,640]{3,2,1,0:T(8,128)S(1)}, f32[2,2,8,640]{3,2,1,0:T(8,128)S(1)}) fusion(f32[1,8,8,640]{3,2,1,0:T(8,128)} %bitcast.59, f32[1,8,8,640]{3,2,1,0:T(8,128)} %bitcast.63), kind=kLoop, calls=%fused_computation.82 | loop fusion | flops 40960 | bytes 491520 | tf_op jit(solution)/shard_map/stack | solution.py:73
  1.6 2.5 %collective-permute-start.1 = (f32[2,2,8,640]{3,2,1,0:T(8,128)S(1)}, f32[2,2,8,640]{3,2,1,0:T(8,128)S(1)}, u32[]{:S(2)}, u32[]{:S(2)}) collective-permute-start(f32[2,2,8,640]{3,2,1,0:T(8,128)S(1)} %get-tuple-element.72), channel_id=1, source_target_pairs={{8,0},{16,8},{24,16},{0,24},{9,1},{17,9},{25,17},{1,25},{10,2},{18... | collective-permute-start | bytes 245768 | tf_op jit(solution)/shard_map/ppermute | solution.py:16
  4.2 1.7 %reshape.154 = s32[10,4096]{1,0:T(8,128)} reshape(s32[8,8,640]{2,1,0:T(8,128)} %param.13) | data formatting | bytes 327680 | tf_op jit(solution)/shard_map/reshape | solution.py:119
  5.9 0.9 %convert_reduce_fusion = s32[32]{0:T(128)S(1)} fusion(s32[32]{0:T(128)} %bitcast.70), kind=kLoop, calls=%fused_computation.112 | loop fusion | flops 5088 | bytes 256 | tf_op jit(solution)/shard_map/reduce_sum | solution.py:62
  7.5 0.9 %convert_reduce_fusion.1 = s32[32]{0:T(128)S(1)} fusion(s32[32]{0:T(128)} %bitcast.71), kind=kLoop, calls=%fused_computation.113 | loop fusion | flops 5088 | bytes 256 | tf_op jit(solution)/shard_map/reduce_sum | solution.py:62
  9.0 1.2 %pad_maximum_fusion.1 = (f32[2,10,8,640]{3,2,1,0:T(8,128)S(1)}, f32[2,10,8,640]{3,2,1,0:T(8,128)S(1)}) fusion(f32[2,2,8,640]{3,2,1,0:T(8,128)S(1)} %collective-permute-done.1, f32[1,8,8,640]{3,2,1,0:T(8,128)} %bitcast.60, f32[1,8,8,640]{3,2,1,0:T(8,128)} %bitcast.64, f32[2,2,8,640]{3,2,1,0:T(8,128)S(1)} %collective-permute-done), kind=kLoop, calls=%fused_computation.12 | loop fusion | flops 409600 | bytes 1310720 | tf_op jit(solution)/shard_map/concatenate | solution.py:17
  10.3 1.0 %fusion.16 = f32[10,8,640]{2,1,0:T(8,128)S(1)} fusion(f32[2,10,8,640]{3,2,1,0:T(8,128)S(1)} %get-tuple-element.71, f32[2,10,8,640]{3,2,1,0:T(8,128)S(1)} %get-tuple-element.70, f32[2,2,8,640]{3,2,1,0:T(8,128)S(1)} %collective-permute-done.1, f32[1,8,8,640]{3,2,1,0:T(8,128)} %bitcast.61, f32[1,8,8,640]{3,2,1,0:T(8,128)} %bitcast.65, ...), kind=kLoop, calls=%fused_computation.42 | loop fusion | flops 563200 | bytes 1105920 | tf_op jit(solution)/shard_map/min | solution.py:29
  11.5 3.4 %collective-permute-start.2 = (f32[2,8,2,640]{3,2,1,0:T(2,128)S(1)}, f32[2,8,2,640]{3,2,1,0:T(2,128)S(1)}, u32[]{:S(2)}, u32[]{:S(2)}) collective-permute-start(f32[2,8,2,640]{3,2,1,0:T(2,128)S(1)} %get-tuple-element.68), channel_id=1, source_target_pairs={{0,1},{1,2},{2,3},{3,4},{4,5},{5,6},{6,7},{8,9},{9,10},{10,11},{11... | collective-permute-start | bytes 245768 | tf_op jit(solution)/shard_map/ppermute | solution.py:15
  14.9 1.3 %collective-permute-start.3 = (f32[2,8,2,640]{3,2,1,0:T(2,128)S(1)}, f32[2,8,2,640]{3,2,1,0:T(2,128)S(1)}, u32[]{:S(2)}, u32[]{:S(2)}) collective-permute-start(f32[2,8,2,640]{3,2,1,0:T(2,128)S(1)} %get-tuple-element.69), channel_id=1, source_target_pairs={{1,0},{2,1},{3,2},{4,3},{5,4},{6,5},{7,6},{9,8},{10,9},{11,10},{12... | collective-permute-start | bytes 245768 | tf_op jit(solution)/shard_map/ppermute | solution.py:16
  16.2 1.3 %collective-permute-done.2 = f32[2,8,2,640]{3,2,1,0:T(2,128)S(1)} collective-permute-done((f32[2,8,2,640]{3,2,1,0:T(2,128)S(1)}, f32[2,8,2,640]{3,2,1,0:T(2,128)S(1)}, u32[]{:S(2)}, u32[]{:S(2)}) %collective-permute-start.2) | collective-permute-done | bytes 81952 | tf_op jit(solution)/shard_map/ppermute | solution.py:15
  17.5 4.1 %collective-permute-done.3 = f32[2,8,2,640]{3,2,1,0:T(2,128)S(1)} collective-permute-done((f32[2,8,2,640]{3,2,1,0:T(2,128)S(1)}, f32[2,8,2,640]{3,2,1,0:T(2,128)S(1)}, u32[]{:S(2)}, u32[]{:S(2)}) %collective-permute-start.3) | collective-permute-done | bytes 81952 | tf_op jit(solution)/shard_map/ppermute | solution.py:16
  22.8 0.9 %broadcast_multiply_fusion.1 = (f32[8,8,640]{2,1,0:T(8,128)S(1)}, f32[8,8,640]{2,1,0:T(8,128)S(1)}, f32[8,8,640]{2,1,0:T(8,128)S(1)}, f32[8,8,640]{2,1,0:T(8,128...) fusion(f32[8,8,640]{2,1,0:T(8,128)S(1)} %get-tuple-element.65, ...), kind=kLoop, calls=%fused_computation.85 | loop fusion | flops 819200 | bytes 3302784 | tf_op jit(solution)/shard_map/mul | solution.py:117
  23.7 0.7 constant_dynamic-update-slice_fusion.12
  25.0 0.7 constant_dynamic-update-slice_fusion.11
  25.7 0.7 constant_dynamic-update-slice_fusion.10
  26.4 0.7 constant_dynamic-update-slice_fusion.9
  27.2 0.7 constant_dynamic-update-slice_fusion.8
  27.9 0.7 constant_dynamic-update-slice_fusion.7
  28.6 0.7 constant_dynamic-update-slice_fusion.6
  29.4 0.7 constant_dynamic-update-slice_fusion.5
  30.1 0.7 constant_dynamic-update-slice_fusion.4
  30.8 0.7 constant_dynamic-update-slice_fusion.3
  31.6 0.7 constant_dynamic-update-slice_fusion.2
  32.3 0.7 constant_dynamic-update-slice_fusion.1
  33.7 30.6 %while.11 = (s32[]{:T(128)}, f32[13,32]{1,0:T(8,128)S(1)}, f32[10,13,4096]{2,0,1:T(8,128)}, s32[10,4096]{1,0:T(8,128)}, s32[]{:T(128)}, /*index=5*/s32[]{:T(128)}) while((s32[]{:T(128)}, f32[13,32]{1,0:T(8,128)S(1)}, f32[10,13,4096]{2,0,1:T(8,128)}, s32[10,4096]{1,0:T(8,128)}, s32[]{:T(128)}, /*index=5*/s32[]{:T(128)}) %tuple.55), condition=%wide.region_1.2_spmd.clone, body=%wide.region_0.1_spmd.clone.sunk | while | flops 20579140 | bytes 691543 | solution.py:127
  33.7 1.6 %constant_dynamic-slice_fusion.4 = f32[1,13,4096]{2,0,1:T(1,128)S(1)} fusion(f32[10,13,4096]{2,0,1:T(8,128)} %get-tuple-element.143, s32[]{:T(128)} %get-tuple-element.135), kind=kLoop, calls=%fused_computation.6.clone.1 | loop fusion | bytes 425988 | tf_op jit(solution)/shard_map/while/body/jit(dynamic_index_in_dim)/dynamic_slice | solution.py:127
  35.4 0.9 %constant_dynamic-slice_fusion.5 = s32[1,4096]{1,0:T(1,128)S(1)} fusion(s32[10,4096]{1,0:T(8,128)} %get-tuple-element.144, s32[]{:T(128)} %get-tuple-element.135), kind=kLoop, calls=%fused_computation.5.clone.1 | loop fusion | bytes 32772 | tf_op jit(solution)/shard_map/while/body/jit(dynamic_index_in_dim)/dynamic_slice | solution.py:127
  36.8 1.6 %constant_dynamic-slice_fusion.4 = f32[1,13,4096]{2,0,1:T(1,128)S(1)} fusion(f32[10,13,4096]{2,0,1:T(8,128)} %get-tuple-element.143, s32[]{:T(128)} %get-tuple-element.135), kind=kLoop, calls=%fused_computation.6.clone.1 | loop fusion | bytes 425988 | tf_op jit(solution)/shard_map/while/body/jit(dynamic_index_in_dim)/dynamic_slice | solution.py:127
  38.5 0.9 %constant_dynamic-slice_fusion.5 = s32[1,4096]{1,0:T(1,128)S(1)} fusion(s32[10,4096]{1,0:T(8,128)} %get-tuple-element.144, s32[]{:T(128)} %get-tuple-element.135), kind=kLoop, calls=%fused_computation.5.clone.1 | loop fusion | bytes 32772 | tf_op jit(solution)/shard_map/while/body/jit(dynamic_index_in_dim)/dynamic_slice | solution.py:127
  39.9 1.6 %constant_dynamic-slice_fusion.4 = f32[1,13,4096]{2,0,1:T(1,128)S(1)} fusion(f32[10,13,4096]{2,0,1:T(8,128)} %get-tuple-element.143, s32[]{:T(128)} %get-tuple-element.135), kind=kLoop, calls=%fused_computation.6.clone.1 | loop fusion | bytes 425988 | tf_op jit(solution)/shard_map/while/body/jit(dynamic_index_in_dim)/dynamic_slice | solution.py:127
  41.5 0.9 %constant_dynamic-slice_fusion.5 = s32[1,4096]{1,0:T(1,128)S(1)} fusion(s32[10,4096]{1,0:T(8,128)} %get-tuple-element.144, s32[]{:T(128)} %get-tuple-element.135), kind=kLoop, calls=%fused_computation.5.clone.1 | loop fusion | bytes 32772 | tf_op jit(solution)/shard_map/while/body/jit(dynamic_index_in_dim)/dynamic_slice | solution.py:127
  42.9 1.6 %constant_dynamic-slice_fusion.4 = f32[1,13,4096]{2,0,1:T(1,128)S(1)} fusion(f32[10,13,4096]{2,0,1:T(8,128)} %get-tuple-element.143, s32[]{:T(128)} %get-tuple-element.135), kind=kLoop, calls=%fused_computation.6.clone.1 | loop fusion | bytes 425988 | tf_op jit(solution)/shard_map/while/body/jit(dynamic_index_in_dim)/dynamic_slice | solution.py:127
  44.6 0.9 %constant_dynamic-slice_fusion.5 = s32[1,4096]{1,0:T(1,128)S(1)} fusion(s32[10,4096]{1,0:T(8,128)} %get-tuple-element.144, s32[]{:T(128)} %get-tuple-element.135), kind=kLoop, calls=%fused_computation.5.clone.1 | loop fusion | bytes 32772 | tf_op jit(solution)/shard_map/while/body/jit(dynamic_index_in_dim)/dynamic_slice | solution.py:127
  46.0 1.6 %constant_dynamic-slice_fusion.4 = f32[1,13,4096]{2,0,1:T(1,128)S(1)} fusion(f32[10,13,4096]{2,0,1:T(8,128)} %get-tuple-element.143, s32[]{:T(128)} %get-tuple-element.135), kind=kLoop, calls=%fused_computation.6.clone.1 | loop fusion | bytes 425988 | tf_op jit(solution)/shard_map/while/body/jit(dynamic_index_in_dim)/dynamic_slice | solution.py:127
  47.7 0.9 %constant_dynamic-slice_fusion.5 = s32[1,4096]{1,0:T(1,128)S(1)} fusion(s32[10,4096]{1,0:T(8,128)} %get-tuple-element.144, s32[]{:T(128)} %get-tuple-element.135), kind=kLoop, calls=%fused_computation.5.clone.1 | loop fusion | bytes 32772 | tf_op jit(solution)/shard_map/while/body/jit(dynamic_index_in_dim)/dynamic_slice | solution.py:127
  49.1 1.6 %constant_dynamic-slice_fusion.4 = f32[1,13,4096]{2,0,1:T(1,128)S(1)} fusion(f32[10,13,4096]{2,0,1:T(8,128)} %get-tuple-element.143, s32[]{:T(128)} %get-tuple-element.135), kind=kLoop, calls=%fused_computation.6.clone.1 | loop fusion | bytes 425988 | tf_op jit(solution)/shard_map/while/body/jit(dynamic_index_in_dim)/dynamic_slice | solution.py:127
  50.7 0.9 %constant_dynamic-slice_fusion.5 = s32[1,4096]{1,0:T(1,128)S(1)} fusion(s32[10,4096]{1,0:T(8,128)} %get-tuple-element.144, s32[]{:T(128)} %get-tuple-element.135), kind=kLoop, calls=%fused_computation.5.clone.1 | loop fusion | bytes 32772 | tf_op jit(solution)/shard_map/while/body/jit(dynamic_index_in_dim)/dynamic_slice | solution.py:127
  52.1 1.6 %constant_dynamic-slice_fusion.4 = f32[1,13,4096]{2,0,1:T(1,128)S(1)} fusion(f32[10,13,4096]{2,0,1:T(8,128)} %get-tuple-element.143, s32[]{:T(128)} %get-tuple-element.135), kind=kLoop, calls=%fused_computation.6.clone.1 | loop fusion | bytes 425988 | tf_op jit(solution)/shard_map/while/body/jit(dynamic_index_in_dim)/dynamic_slice | solution.py:127
  53.8 0.9 %constant_dynamic-slice_fusion.5 = s32[1,4096]{1,0:T(1,128)S(1)} fusion(s32[10,4096]{1,0:T(8,128)} %get-tuple-element.144, s32[]{:T(128)} %get-tuple-element.135), kind=kLoop, calls=%fused_computation.5.clone.1 | loop fusion | bytes 32772 | tf_op jit(solution)/shard_map/while/body/jit(dynamic_index_in_dim)/dynamic_slice | solution.py:127
  55.2 1.6 %constant_dynamic-slice_fusion.4 = f32[1,13,4096]{2,0,1:T(1,128)S(1)} fusion(f32[10,13,4096]{2,0,1:T(8,128)} %get-tuple-element.143, s32[]{:T(128)} %get-tuple-element.135), kind=kLoop, calls=%fused_computation.6.clone.1 | loop fusion | bytes 425988 | tf_op jit(solution)/shard_map/while/body/jit(dynamic_index_in_dim)/dynamic_slice | solution.py:127
  56.9 0.9 %constant_dynamic-slice_fusion.5 = s32[1,4096]{1,0:T(1,128)S(1)} fusion(s32[10,4096]{1,0:T(8,128)} %get-tuple-element.144, s32[]{:T(128)} %get-tuple-element.135), kind=kLoop, calls=%fused_computation.5.clone.1 | loop fusion | bytes 32772 | tf_op jit(solution)/shard_map/while/body/jit(dynamic_index_in_dim)/dynamic_slice | solution.py:127
  58.3 1.6 %constant_dynamic-slice_fusion.4 = f32[1,13,4096]{2,0,1:T(1,128)S(1)} fusion(f32[10,13,4096]{2,0,1:T(8,128)} %get-tuple-element.143, s32[]{:T(128)} %get-tuple-element.135), kind=kLoop, calls=%fused_computation.6.clone.1 | loop fusion | bytes 425988 | tf_op jit(solution)/shard_map/while/body/jit(dynamic_index_in_dim)/dynamic_slice | solution.py:127
  59.9 0.9 %constant_dynamic-slice_fusion.5 = s32[1,4096]{1,0:T(1,128)S(1)} fusion(s32[10,4096]{1,0:T(8,128)} %get-tuple-element.144, s32[]{:T(128)} %get-tuple-element.135), kind=kLoop, calls=%fused_computation.5.clone.1 | loop fusion | bytes 32772 | tf_op jit(solution)/shard_map/while/body/jit(dynamic_index_in_dim)/dynamic_slice | solution.py:127
  61.3 1.6 %constant_dynamic-slice_fusion.4 = f32[1,13,4096]{2,0,1:T(1,128)S(1)} fusion(f32[10,13,4096]{2,0,1:T(8,128)} %get-tuple-element.143, s32[]{:T(128)} %get-tuple-element.135), kind=kLoop, calls=%fused_computation.6.clone.1 | loop fusion | bytes 425988 | tf_op jit(solution)/shard_map/while/body/jit(dynamic_index_in_dim)/dynamic_slice | solution.py:127
  63.0 0.9 %constant_dynamic-slice_fusion.5 = s32[1,4096]{1,0:T(1,128)S(1)} fusion(s32[10,4096]{1,0:T(8,128)} %get-tuple-element.144, s32[]{:T(128)} %get-tuple-element.135), kind=kLoop, calls=%fused_computation.5.clone.1 | loop fusion | bytes 32772 | tf_op jit(solution)/shard_map/while/body/jit(dynamic_index_in_dim)/dynamic_slice | solution.py:127
  64.4 20.1 %psum.7 = f32[13,32]{1,0:T(8,128)S(1)} all-reduce(f32[13,32]{1,0:T(8,128)S(1)} %get-tuple-element.30), channel_id=1, replica_groups=mesh['px'=4,'py'=8] {'py'}, use_global_device_ids=true, to_apply=%region_2.3 | all-reduce | flops 416 | bytes 3328 | tf_op jit(solution)/shard_map/psum | solution.py:133
  84.6 0.8 convolution_bitcast_fusion.1
  85.5 0.8 convolution_bitcast_fusion
  (62 shorter events, 8.8 us)
Async XLA Ops:
  0.6 10.6 %copy-start.1 = (f32[8,8,640]{2,1,0:T(8,128)S(1)}, f32[8,8,640]{2,1,0:T(8,128)}, u32[]{:S(2)}) copy-start(f32[8,8,640]{2,1,0:T(8,128)} %param.9) | copy-start | bytes 491524
  0.6 10.6 %copy-start = (f32[8,8,640]{2,1,0:T(8,128)S(1)}, f32[8,8,640]{2,1,0:T(8,128)}, u32[]{:S(2)}) copy-start(f32[8,8,640]{2,1,0:T(8,128)} %param.10) | copy-start | bytes 491524
  0.7 10.8 %copy-start.4 = (f32[8,8,640]{2,1,0:T(8,128)S(1)}, f32[8,8,640]{2,1,0:T(8,128)}, u32[]{:S(2)}) copy-start(f32[8,8,640]{2,1,0:T(8,128)} %param.11) | copy-start | bytes 491524
  1.6 7.5 %collective-permute-start.1 = (f32[2,2,8,640]{3,2,1,0:T(8,128)S(1)}, f32[2,2,8,640]{3,2,1,0:T(8,128)S(1)}, u32[]{:S(2)}, u32[]{:S(2)}) collective-permute-start(f32[2,2,8,640]{3,2,1,0:T(8,128)S(1)} %get-tuple-element.72), channel_id=1, source_target_pairs={{8,0},{16,8},{24,16},{0,24},{9,1},{17,9},{25,17},{1,25},{10,2},{18... | collective-permute-start | bytes 245768 | tf_op jit(solution)/shard_map/ppermute | solution.py:16
  4.0 5.0 %collective-permute-start = (f32[2,2,8,640]{3,2,1,0:T(8,128)S(1)}, f32[2,2,8,640]{3,2,1,0:T(8,128)S(1)}, u32[]{:S(2)}, u32[]{:S(2)}) collective-permute-start(f32[2,2,8,640]{3,2,1,0:T(8,128)S(1)} %get-tuple-element.73), channel_id=1, source_target_pairs={{0,8},{8,16},{16,24},{24,0},{1,9},{9,17},{17,25},{25,1},{2,10},{10... | collective-permute-start | bytes 245768 | tf_op jit(solution)/shard_map/ppermute | solution.py:15
  11.5 6.0 %collective-permute-start.2 = (f32[2,8,2,640]{3,2,1,0:T(2,128)S(1)}, f32[2,8,2,640]{3,2,1,0:T(2,128)S(1)}, u32[]{:S(2)}, u32[]{:S(2)}) collective-permute-start(f32[2,8,2,640]{3,2,1,0:T(2,128)S(1)} %get-tuple-element.68), channel_id=1, source_target_pairs={{0,1},{1,2},{2,3},{3,4},{4,5},{5,6},{6,7},{8,9},{9,10},{10,11},{11... | collective-permute-start | bytes 245768 | tf_op jit(solution)/shard_map/ppermute | solution.py:15
  14.9 6.7 %collective-permute-start.3 = (f32[2,8,2,640]{3,2,1,0:T(2,128)S(1)}, f32[2,8,2,640]{3,2,1,0:T(2,128)S(1)}, u32[]{:S(2)}, u32[]{:S(2)}) collective-permute-start(f32[2,8,2,640]{3,2,1,0:T(2,128)S(1)} %get-tuple-element.69), channel_id=1, source_target_pairs={{1,0},{2,1},{3,2},{4,3},{5,4},{6,5},{7,6},{9,8},{10,9},{11,10},{12... | collective-permute-start | bytes 245768 | tf_op jit(solution)/shard_map/ppermute | solution.py:16
  16.2 6.2 %copy-start.2 = (f32[8,8,640]{2,1,0:T(8,128)S(1)}, f32[8,8,640]{2,1,0:T(8,128)}, u32[]{:S(2)}) copy-start(f32[8,8,640]{2,1,0:T(8,128)} %param.12) | copy-start | bytes 491524
  21.8 1.0 %copy-start.3 = (s32[8,8,640]{2,1,0:T(8,128)S(1)}, s32[8,8,640]{2,1,0:T(8,128)}, u32[]{:S(2)}) copy-start(s32[8,8,640]{2,1,0:T(8,128)} %param.13) | copy-start | bytes 491524
where the time goes:
time: 87.1 us; the launch traced here: 86.4 us
  local copies, waits for them, and re-layouts  37.5 us (43%)
  blocking collectives  20.1 us (23%)
  other arithmetic  8.61 us (10%)
  starting transfers between devices  7.18 us (8%)
  matrix products  6.3 us (7%)
  waiting for transfers between devices  5.37 us (6%)
  between operations  0.97 us (1%)
    dynamic_slice x20, local copies, waits for them, and re-layouts, local(): lax.scan(accumulate, jnp.zeros((13, structures), jnp.float32), (feature_b...  25.7 us
    psum x1, blocking collectives, local(): totals = lax.psum(partial_sums, 'py')  20.1 us
    unnamed x22, local copies, waits for them, and re-layouts  8.8 us
    dot_general x12, matrix products, product(): jnp.dot(left, right, precision=lax.Precision.HIGHEST, preferred_element_t...  6.3 us
    ppermute x2, waiting for transfers between devices, with_halo(): after = lax.ppermute(initial, axis, down)  4.12 us
    ppermute x2, starting transfers between devices, with_halo(): after = lax.ppermute(initial, axis, down)  3.75 us
    ppermute x2, starting transfers between devices, with_halo(): before = lax.ppermute(last, axis, up)  3.43 us
    reduce_sum x2, other arithmetic, slot_table(): rank = jnp.sum((same & earlier).astype(jnp.int32), axis=1)  1.82 us
  transfers between devices with their start and end apart: 4, of which 2 were waited for; matrix products, arithmetic and copies ran while one was open for 6% of the time, Pallas kernels for 0%

commit v1 on v0

--- a/solution.py
+++ b/solution.py
@@ -130,7 +130,9 @@
     owner_slots = slot_table(structure_owner[0], per_owner)
     parcel_slots = slot_table(parcel_owner[0], per_owner)
     mine_owned = lax.dynamic_slice_in_dim(owner_slots, row_index * per_owner, per_owner, 1)
-    totals = lax.psum(partial_sums, "py")
+    totals = partial_sums
+    for hop in (1, 2, 4):
+        totals = totals + lax.ppermute(totals, "py", [(dev, dev ^ hop) for dev in range(8)])
     owned = product(totals, mine_owned)
     mine_parcels = lax.dynamic_slice_in_dim(parcel_slots, row_index * per_owner, per_owner, 1)
     received = product(parcel_rows(totals), mine_parcels)

time: 87.1 us -> 77.6 us (0.89)
  blocking collectives: 20.1 us -> 0 us
  starting transfers between devices: 7.18 us -> 13.8 us
  waiting for transfers between devices: 5.37 us -> 11.6 us
  other arithmetic: 8.61 us -> 6.56 us
    psum x1 -> x0, blocking collectives: 20.1 us -> none  [local(): totals = lax.psum(partial_sums, 'py')]
    ppermute x0 -> x3, starting transfers between devices: none -> 6.64 us  [local(): lax.ppermute(totals, 'py', [(dev, dev ^ hop) for dev in range(8)])]
    ppermute x0 -> x3, waiting for transfers between devices: none -> 5.49 us  [local(): lax.ppermute(totals, 'py', [(dev, dev ^ hop) for dev in range(8)])]
    add x2, other arithmetic: 1.33 us -> 0.01 us  [slot_table(): position = owner_row * per_owner + rank]
    unnamed x22 -> x26, local copies, waits for them, and re-layouts: 8.8 us -> 8.67 us
  transfers between devices with their start and end apart: 4 -> 7, of which waited for: 2 -> 6; matrix products, arithmetic and copies ran while one was open for 6% -> 4% of each run, Pallas kernels for 0% -> 0%
where the time goes in v1:
time: 77.6 us; the launch traced here: 76.9 us
  local copies, waits for them, and re-layouts  37.3 us (48%)
  starting transfers between devices  13.8 us (18%)
  waiting for transfers between devices  11.6 us (15%)
  other arithmetic  6.56 us (8%)
  matrix products  6.3 us (8%)
  between operations  0.95 us (1%)
    dynamic_slice x20, local copies, waits for them, and re-layouts, local(): lax.scan(accumulate, jnp.zeros((13, structures), jnp.float32), (feature_b...  25.7 us
    unnamed x26, local copies, waits for them, and re-layouts  8.67 us
    ppermute x3, starting transfers between devices, local(): lax.ppermute(totals, 'py', [(dev, dev ^ hop) for dev in range(8)])  6.64 us
    dot_general x12, matrix products, product(): jnp.dot(left, right, precision=lax.Precision.HIGHEST, preferred_element_t...  6.3 us
    ppermute x3, waiting for transfers between devices, local(): lax.ppermute(totals, 'py', [(dev, dev ^ hop) for dev in range(8)])  5.49 us
    ppermute x2, waiting for transfers between devices, with_halo(): after = lax.ppermute(initial, axis, down)  4.31 us
    ppermute x2, starting transfers between devices, with_halo(): after = lax.ppermute(initial, axis, down)  3.75 us
    ppermute x2, starting transfers between devices, with_halo(): before = lax.ppermute(last, axis, up)  3.43 us
  transfers between devices with their start and end apart: 7, of which 6 were waited for; matrix products, arithmetic and copies ran while one was open for 4% of the time, Pallas kernels for 0%

profile of v1, /device:TPU:0, one launch (start us, length us, event | category | flops | bytes accessed | tf_op | source)
XLA Modules:
  0.0 76.9 jit_solution(15022045857597489059)
XLA Ops:
  0.7 0.9 %pad_maximum_fusion.7 = (f32[2,2,8,640]{3,2,1,0:T(8,128)S(1)}, f32[2,2,8,640]{3,2,1,0:T(8,128)S(1)}) fusion(f32[1,8,8,640]{3,2,1,0:T(8,128)} %bitcast.59, f32[1,8,8,640]{3,2,1,0:T(8,128)} %bitcast.63), kind=kLoop, calls=%fused_computation.82 | loop fusion | flops 40960 | bytes 491520 | tf_op jit(solution)/shard_map/stack | solution.py:73
  1.6 2.5 %collective-permute-start.1 = (f32[2,2,8,640]{3,2,1,0:T(8,128)S(1)}, f32[2,2,8,640]{3,2,1,0:T(8,128)S(1)}, u32[]{:S(2)}, u32[]{:S(2)}) collective-permute-start(f32[2,2,8,640]{3,2,1,0:T(8,128)S(1)} %get-tuple-element.72), channel_id=1, source_target_pairs={{8,0},{16,8},{24,16},{0,24},{9,1},{17,9},{25,17},{1,25},{10,2},{18... | collective-permute-start | bytes 245768 | tf_op jit(solution)/shard_map/ppermute | solution.py:16
  4.2 1.7 %reshape.154 = s32[10,4096]{1,0:T(8,128)} reshape(s32[8,8,640]{2,1,0:T(8,128)} %param.13) | data formatting | bytes 327680 | tf_op jit(solution)/shard_map/reshape | solution.py:119
  5.9 0.9 %convert_reduce_fusion = s32[32]{0:T(128)S(1)} fusion(s32[32]{0:T(128)} %bitcast.70), kind=kLoop, calls=%fused_computation.112 | loop fusion | flops 5088 | bytes 256 | tf_op jit(solution)/shard_map/reduce_sum | solution.py:62
  6.8 1.1 %collective-permute-done = f32[2,2,8,640]{3,2,1,0:T(8,128)S(1)} collective-permute-done((f32[2,2,8,640]{3,2,1,0:T(8,128)S(1)}, f32[2,2,8,640]{3,2,1,0:T(8,128)S(1)}, u32[]{:S(2)}, u32[]{:S(2)}) %collective-permute-start) | collective-permute-done | bytes 81952 | tf_op jit(solution)/shard_map/ppermute | solution.py:15
  7.9 1.2 %pad_maximum_fusion.1 = (f32[2,10,8,640]{3,2,1,0:T(8,128)S(1)}, f32[2,10,8,640]{3,2,1,0:T(8,128)S(1)}) fusion(f32[2,2,8,640]{3,2,1,0:T(8,128)S(1)} %collective-permute-done.1, f32[1,8,8,640]{3,2,1,0:T(8,128)} %bitcast.60, f32[1,8,8,640]{3,2,1,0:T(8,128)} %bitcast.64, f32[2,2,8,640]{3,2,1,0:T(8,128)S(1)} %collective-permute-done), kind=kLoop, calls=%fused_computation.12 | loop fusion | flops 409600 | bytes 1310720 | tf_op jit(solution)/shard_map/concatenate | solution.py:17
  9.1 1.0 %fusion.16 = f32[10,8,640]{2,1,0:T(8,128)S(1)} fusion(f32[2,10,8,640]{3,2,1,0:T(8,128)S(1)} %get-tuple-element.71, f32[2,10,8,640]{3,2,1,0:T(8,128)S(1)} %get-tuple-element.70, f32[2,2,8,640]{3,2,1,0:T(8,128)S(1)} %collective-permute-done.1, f32[1,8,8,640]{3,2,1,0:T(8,128)} %bitcast.61, f32[1,8,8,640]{3,2,1,0:T(8,128)} %bitcast.65, ...), kind=kLoop, calls=%fused_computation.42 | loop fusion | flops 563200 | bytes 1105920 | tf_op jit(solution)/shard_map/min | solution.py:29
  10.3 3.4 %collective-permute-start.2 = (f32[2,8,2,640]{3,2,1,0:T(2,128)S(1)}, f32[2,8,2,640]{3,2,1,0:T(2,128)S(1)}, u32[]{:S(2)}, u32[]{:S(2)}) collective-permute-start(f32[2,8,2,640]{3,2,1,0:T(2,128)S(1)} %get-tuple-element.68), channel_id=1, source_target_pairs={{0,1},{1,2},{2,3},{3,4},{4,5},{5,6},{6,7},{8,9},{9,10},{10,11},{11... | collective-permute-start | bytes 245768 | tf_op jit(solution)/shard_map/ppermute | solution.py:15
  13.8 1.3 %collective-permute-start.3 = (f32[2,8,2,640]{3,2,1,0:T(2,128)S(1)}, f32[2,8,2,640]{3,2,1,0:T(2,128)S(1)}, u32[]{:S(2)}, u32[]{:S(2)}) collective-permute-start(f32[2,8,2,640]{3,2,1,0:T(2,128)S(1)} %get-tuple-element.69), channel_id=1, source_target_pairs={{1,0},{2,1},{3,2},{4,3},{5,4},{6,5},{7,6},{9,8},{10,9},{11,10},{12... | collective-permute-start | bytes 245768 | tf_op jit(solution)/shard_map/ppermute | solution.py:16
  15.8 4.3 %collective-permute-done.3 = f32[2,8,2,640]{3,2,1,0:T(2,128)S(1)} collective-permute-done((f32[2,8,2,640]{3,2,1,0:T(2,128)S(1)}, f32[2,8,2,640]{3,2,1,0:T(2,128)S(1)}, u32[]{:S(2)}, u32[]{:S(2)}) %collective-permute-start.3) | collective-permute-done | bytes 81952 | tf_op jit(solution)/shard_map/ppermute | solution.py:16
  21.3 0.9 %broadcast_multiply_fusion.1 = (f32[8,8,640]{2,1,0:T(8,128)S(1)}, f32[8,8,640]{2,1,0:T(8,128)S(1)}, f32[8,8,640]{2,1,0:T(8,128)S(1)}, f32[8,8,640]{2,1,0:T(8,128...) fusion(f32[8,8,640]{2,1,0:T(8,128)S(1)} %get-tuple-element.65, ...), kind=kLoop, calls=%fused_computation.85 | loop fusion | flops 819200 | bytes 3302784 | tf_op jit(solution)/shard_map/mul | solution.py:117
  22.2 0.7 constant_dynamic-update-slice_fusion.12
  23.5 0.7 constant_dynamic-update-slice_fusion.11
  24.9 0.7 constant_dynamic-update-slice_fusion.9
  27.0 0.7 constant_dynamic-update-slice_fusion.6
  28.5 0.7 constant_dynamic-update-slice_fusion.4
  29.2 0.7 constant_dynamic-update-slice_fusion.3
  29.9 0.7 constant_dynamic-update-slice_fusion.2
  30.7 0.7 constant_dynamic-update-slice_fusion.1
  32.1 30.6 %while.11 = (s32[]{:T(128)}, f32[13,32]{1,0:T(8,128)S(1)}, f32[10,13,4096]{2,0,1:T(8,128)}, s32[10,4096]{1,0:T(8,128)}, s32[]{:T(128)}, /*index=5*/s32[]{:T(128)}) while((s32[]{:T(128)}, f32[13,32]{1,0:T(8,128)S(1)}, f32[10,13,4096]{2,0,1:T(8,128)}, s32[10,4096]{1,0:T(8,128)}, s32[]{:T(128)}, /*index=5*/s32[]{:T(128)}) %tuple.55), condition=%wide.region_1.2_spmd.clone, body=%wide.region_0.1_spmd.clone.sunk | while | flops 20579140 | bytes 691543 | solution.py:127
  32.1 1.6 %constant_dynamic-slice_fusion.4 = f32[1,13,4096]{2,0,1:T(1,128)S(1)} fusion(f32[10,13,4096]{2,0,1:T(8,128)} %get-tuple-element.143, s32[]{:T(128)} %get-tuple-element.135), kind=kLoop, calls=%fused_computation.6.clone.1 | loop fusion | bytes 425988 | tf_op jit(solution)/shard_map/while/body/jit(dynamic_index_in_dim)/dynamic_slice | solution.py:127
  33.7 0.9 %constant_dynamic-slice_fusion.5 = s32[1,4096]{1,0:T(1,128)S(1)} fusion(s32[10,4096]{1,0:T(8,128)} %get-tuple-element.144, s32[]{:T(128)} %get-tuple-element.135), kind=kLoop, calls=%fused_computation.5.clone.1 | loop fusion | bytes 32772 | tf_op jit(solution)/shard_map/while/body/jit(dynamic_index_in_dim)/dynamic_slice | solution.py:127
  35.1 1.6 %constant_dynamic-slice_fusion.4 = f32[1,13,4096]{2,0,1:T(1,128)S(1)} fusion(f32[10,13,4096]{2,0,1:T(8,128)} %get-tuple-element.143, s32[]{:T(128)} %get-tuple-element.135), kind=kLoop, calls=%fused_computation.6.clone.1 | loop fusion | bytes 425988 | tf_op jit(solution)/shard_map/while/body/jit(dynamic_index_in_dim)/dynamic_slice | solution.py:127
  36.8 0.9 %constant_dynamic-slice_fusion.5 = s32[1,4096]{1,0:T(1,128)S(1)} fusion(s32[10,4096]{1,0:T(8,128)} %get-tuple-element.144, s32[]{:T(128)} %get-tuple-element.135), kind=kLoop, calls=%fused_computation.5.clone.1 | loop fusion | bytes 32772 | tf_op jit(solution)/shard_map/while/body/jit(dynamic_index_in_dim)/dynamic_slice | solution.py:127
  38.2 1.6 %constant_dynamic-slice_fusion.4 = f32[1,13,4096]{2,0,1:T(1,128)S(1)} fusion(f32[10,13,4096]{2,0,1:T(8,128)} %get-tuple-element.143, s32[]{:T(128)} %get-tuple-element.135), kind=kLoop, calls=%fused_computation.6.clone.1 | loop fusion | bytes 425988 | tf_op jit(solution)/shard_map/while/body/jit(dynamic_index_in_dim)/dynamic_slice | solution.py:127
  39.9 0.9 %constant_dynamic-slice_fusion.5 = s32[1,4096]{1,0:T(1,128)S(1)} fusion(s32[10,4096]{1,0:T(8,128)} %get-tuple-element.144, s32[]{:T(128)} %get-tuple-element.135), kind=kLoop, calls=%fused_computation.5.clone.1 | loop fusion | bytes 32772 | tf_op jit(solution)/shard_map/while/body/jit(dynamic_index_in_dim)/dynamic_slice | solution.py:127
  41.3 1.6 %constant_dynamic-slice_fusion.4 = f32[1,13,4096]{2,0,1:T(1,128)S(1)} fusion(f32[10,13,4096]{2,0,1:T(8,128)} %get-tuple-element.143, s32[]{:T(128)} %get-tuple-element.135), kind=kLoop, calls=%fused_computation.6.clone.1 | loop fusion | bytes 425988 | tf_op jit(solution)/shard_map/while/body/jit(dynamic_index_in_dim)/dynamic_slice | solution.py:127
  42.9 0.9 %constant_dynamic-slice_fusion.5 = s32[1,4096]{1,0:T(1,128)S(1)} fusion(s32[10,4096]{1,0:T(8,128)} %get-tuple-element.144, s32[]{:T(128)} %get-tuple-element.135), kind=kLoop, calls=%fused_computation.5.clone.1 | loop fusion | bytes 32772 | tf_op jit(solution)/shard_map/while/body/jit(dynamic_index_in_dim)/dynamic_slice | solution.py:127
  44.4 1.6 %constant_dynamic-slice_fusion.4 = f32[1,13,4096]{2,0,1:T(1,128)S(1)} fusion(f32[10,13,4096]{2,0,1:T(8,128)} %get-tuple-element.143, s32[]{:T(128)} %get-tuple-element.135), kind=kLoop, calls=%fused_computation.6.clone.1 | loop fusion | bytes 425988 | tf_op jit(solution)/shard_map/while/body/jit(dynamic_index_in_dim)/dynamic_slice | solution.py:127
  46.0 0.9 %constant_dynamic-slice_fusion.5 = s32[1,4096]{1,0:T(1,128)S(1)} fusion(s32[10,4096]{1,0:T(8,128)} %get-tuple-element.144, s32[]{:T(128)} %get-tuple-element.135), kind=kLoop, calls=%fused_computation.5.clone.1 | loop fusion | bytes 32772 | tf_op jit(solution)/shard_map/while/body/jit(dynamic_index_in_dim)/dynamic_slice | solution.py:127
  47.4 1.6 %constant_dynamic-slice_fusion.4 = f32[1,13,4096]{2,0,1:T(1,128)S(1)} fusion(f32[10,13,4096]{2,0,1:T(8,128)} %get-tuple-element.143, s32[]{:T(128)} %get-tuple-element.135), kind=kLoop, calls=%fused_computation.6.clone.1 | loop fusion | bytes 425988 | tf_op jit(solution)/shard_map/while/body/jit(dynamic_index_in_dim)/dynamic_slice | solution.py:127
  49.1 0.9 %constant_dynamic-slice_fusion.5 = s32[1,4096]{1,0:T(1,128)S(1)} fusion(s32[10,4096]{1,0:T(8,128)} %get-tuple-element.144, s32[]{:T(128)} %get-tuple-element.135), kind=kLoop, calls=%fused_computation.5.clone.1 | loop fusion | bytes 32772 | tf_op jit(solution)/shard_map/while/body/jit(dynamic_index_in_dim)/dynamic_slice | solution.py:127
  50.5 1.6 %constant_dynamic-slice_fusion.4 = f32[1,13,4096]{2,0,1:T(1,128)S(1)} fusion(f32[10,13,4096]{2,0,1:T(8,128)} %get-tuple-element.143, s32[]{:T(128)} %get-tuple-element.135), kind=kLoop, calls=%fused_computation.6.clone.1 | loop fusion | bytes 425988 | tf_op jit(solution)/shard_map/while/body/jit(dynamic_index_in_dim)/dynamic_slice | solution.py:127
  52.1 0.9 %constant_dynamic-slice_fusion.5 = s32[1,4096]{1,0:T(1,128)S(1)} fusion(s32[10,4096]{1,0:T(8,128)} %get-tuple-element.144, s32[]{:T(128)} %get-tuple-element.135), kind=kLoop, calls=%fused_computation.5.clone.1 | loop fusion | bytes 32772 | tf_op jit(solution)/shard_map/while/body/jit(dynamic_index_in_dim)/dynamic_slice | solution.py:127
  53.6 1.6 %constant_dynamic-slice_fusion.4 = f32[1,13,4096]{2,0,1:T(1,128)S(1)} fusion(f32[10,13,4096]{2,0,1:T(8,128)} %get-tuple-element.143, s32[]{:T(128)} %get-tuple-element.135), kind=kLoop, calls=%fused_computation.6.clone.1 | loop fusion | bytes 425988 | tf_op jit(solution)/shard_map/while/body/jit(dynamic_index_in_dim)/dynamic_slice | solution.py:127
  55.2 0.9 %constant_dynamic-slice_fusion.5 = s32[1,4096]{1,0:T(1,128)S(1)} fusion(s32[10,4096]{1,0:T(8,128)} %get-tuple-element.144, s32[]{:T(128)} %get-tuple-element.135), kind=kLoop, calls=%fused_computation.5.clone.1 | loop fusion | bytes 32772 | tf_op jit(solution)/shard_map/while/body/jit(dynamic_index_in_dim)/dynamic_slice | solution.py:127
  56.6 1.6 %constant_dynamic-slice_fusion.4 = f32[1,13,4096]{2,0,1:T(1,128)S(1)} fusion(f32[10,13,4096]{2,0,1:T(8,128)} %get-tuple-element.143, s32[]{:T(128)} %get-tuple-element.135), kind=kLoop, calls=%fused_computation.6.clone.1 | loop fusion | bytes 425988 | tf_op jit(solution)/shard_map/while/body/jit(dynamic_index_in_dim)/dynamic_slice | solution.py:127
  58.3 0.9 %constant_dynamic-slice_fusion.5 = s32[1,4096]{1,0:T(1,128)S(1)} fusion(s32[10,4096]{1,0:T(8,128)} %get-tuple-element.144, s32[]{:T(128)} %get-tuple-element.135), kind=kLoop, calls=%fused_computation.5.clone.1 | loop fusion | bytes 32772 | tf_op jit(solution)/shard_map/while/body/jit(dynamic_index_in_dim)/dynamic_slice | solution.py:127
  59.7 1.6 %constant_dynamic-slice_fusion.4 = f32[1,13,4096]{2,0,1:T(1,128)S(1)} fusion(f32[10,13,4096]{2,0,1:T(8,128)} %get-tuple-element.143, s32[]{:T(128)} %get-tuple-element.135), kind=kLoop, calls=%fused_computation.6.clone.1 | loop fusion | bytes 425988 | tf_op jit(solution)/shard_map/while/body/jit(dynamic_index_in_dim)/dynamic_slice | solution.py:127
  61.3 0.9 %constant_dynamic-slice_fusion.5 = s32[1,4096]{1,0:T(1,128)S(1)} fusion(s32[10,4096]{1,0:T(8,128)} %get-tuple-element.144, s32[]{:T(128)} %get-tuple-element.135), kind=kLoop, calls=%fused_computation.5.clone.1 | loop fusion | bytes 32772 | tf_op jit(solution)/shard_map/while/body/jit(dynamic_index_in_dim)/dynamic_slice | solution.py:127
  62.7 2.5 %collective-permute-start.4 = (f32[13,32]{1,0:T(8,128)S(1)}, f32[13,32]{1,0:T(8,128)S(1)}, u32[]{:S(2)}, u32[]{:S(2)}) collective-permute-start(f32[13,32]{1,0:T(8,128)S(1)} %get-tuple-element.30), channel_id=1, source_target_pairs={{0,1},{1,0},{2,3},{3,2},{4,5},{5,4},{6,7},{7,6},{8,9},{9,8},{10,11... | collective-permute-start | bytes 5000 | tf_op jit(solution)/shard_map/ppermute | solution.py:135
  65.2 1.6 %collective-permute-done.4 = f32[13,32]{1,0:T(8,128)S(1)} collective-permute-done((f32[13,32]{1,0:T(8,128)S(1)}, f32[13,32]{1,0:T(8,128)S(1)}, u32[]{:S(2)}, u32[]{:S(2)}) %collective-permute-start.4) | collective-permute-done | bytes 1696 | tf_op jit(solution)/shard_map/ppermute | solution.py:135
  66.9 1.6 %collective-permute-start.5 = (f32[13,32]{1,0:T(8,128)S(1)}, f32[13,32]{1,0:T(8,128)S(1)}, u32[]{:S(2)}, u32[]{:S(2)}) collective-permute-start(f32[13,32]{1,0:T(8,128)S(1)} %add.170), channel_id=1, source_target_pairs={{0,2},{1,3},{2,0},{3,1},{4,6},{5,7},{6,4},{7,5},{8,10},{9,11},{10,... | collective-permute-start | bytes 5000 | tf_op jit(solution)/shard_map/ppermute | solution.py:135
  68.6 1.9 %collective-permute-done.5 = f32[13,32]{1,0:T(8,128)S(1)} collective-permute-done((f32[13,32]{1,0:T(8,128)S(1)}, f32[13,32]{1,0:T(8,128)S(1)}, u32[]{:S(2)}, u32[]{:S(2)}) %collective-permute-start.5) | collective-permute-done | bytes 1696 | tf_op jit(solution)/shard_map/ppermute | solution.py:135
  70.5 2.6 %collective-permute-start.6 = (f32[13,32]{1,0:T(8,128)S(1)}, f32[13,32]{1,0:T(8,128)S(1)}, u32[]{:S(2)}, u32[]{:S(2)}) collective-permute-start(f32[13,32]{1,0:T(8,128)S(1)} %add.171), channel_id=1, source_target_pairs={{0,4},{1,5},{2,6},{3,7},{4,0},{5,1},{6,2},{7,3},{8,12},{9,13},{10,... | collective-permute-start | bytes 5000 | tf_op jit(solution)/shard_map/ppermute | solution.py:135
  73.1 2.0 %collective-permute-done.6 = f32[13,32]{1,0:T(8,128)S(1)} collective-permute-done((f32[13,32]{1,0:T(8,128)S(1)}, f32[13,32]{1,0:T(8,128)S(1)}, u32[]{:S(2)}, u32[]{:S(2)}) %collective-permute-start.6) | collective-permute-done | bytes 1696 | tf_op jit(solution)/shard_map/ppermute | solution.py:135
  75.1 0.8 %convolution_bitcast_fusion.1 = f32[1,13,4]{1,2,0:T(4,128)} fusion(f32[13,32]{1,0:T(8,128)S(1)} %add.172, s32[]{:T(128)S(6)} %select_n.24, s32[32]{0:T(128)S(1)} %multiply_add_fusion.1), kind=kOutput, calls=%fused_computation.8 | convolution fusion | flops 20224 | bytes 2004 | tf_op jit(solution)/shard_map/dot_general | solution.py:68
  76.1 0.8 %convolution_bitcast_fusion = f32[1,13,4]{1,2,0:T(4,128)} fusion(f32[13,32]{1,0:T(8,128)S(1)} %concatenate.22, s32[32]{0:T(128)S(1)} %multiply_add_fusion, s32[]{:T(128)S(6)} %select_n.24), kind=kOutput, calls=%fused_computation.7 | convolution fusion | flops 20224 | bytes 2004 | tf_op jit(solution)/shard_map/dot_general | solution.py:68
  (74 shorter events, 11.2 us)
Async XLA Ops:
  0.6 9.5 %copy-start.1 = (f32[8,8,640]{2,1,0:T(8,128)S(1)}, f32[8,8,640]{2,1,0:T(8,128)}, u32[]{:S(2)}) copy-start(f32[8,8,640]{2,1,0:T(8,128)} %param.9) | copy-start | bytes 491524
  0.6 9.5 %copy-start = (f32[8,8,640]{2,1,0:T(8,128)S(1)}, f32[8,8,640]{2,1,0:T(8,128)}, u32[]{:S(2)}) copy-start(f32[8,8,640]{2,1,0:T(8,128)} %param.10) | copy-start | bytes 491524
  0.7 9.6 %copy-start.4 = (f32[8,8,640]{2,1,0:T(8,128)S(1)}, f32[8,8,640]{2,1,0:T(8,128)}, u32[]{:S(2)}) copy-start(f32[8,8,640]{2,1,0:T(8,128)} %param.11) | copy-start | bytes 491524
  1.6 5.2 %collective-permute-start.1 = (f32[2,2,8,640]{3,2,1,0:T(8,128)S(1)}, f32[2,2,8,640]{3,2,1,0:T(8,128)S(1)}, u32[]{:S(2)}, u32[]{:S(2)}) collective-permute-start(f32[2,2,8,640]{3,2,1,0:T(8,128)S(1)} %get-tuple-element.72), channel_id=1, source_target_pairs={{8,0},{16,8},{24,16},{0,24},{9,1},{17,9},{25,17},{1,25},{10,2},{18... | collective-permute-start | bytes 245768 | tf_op jit(solution)/shard_map/ppermute | solution.py:16
  4.0 3.9 %collective-permute-start = (f32[2,2,8,640]{3,2,1,0:T(8,128)S(1)}, f32[2,2,8,640]{3,2,1,0:T(8,128)S(1)}, u32[]{:S(2)}, u32[]{:S(2)}) collective-permute-start(f32[2,2,8,640]{3,2,1,0:T(8,128)S(1)} %get-tuple-element.73), channel_id=1, source_target_pairs={{0,8},{8,16},{16,24},{24,0},{1,9},{9,17},{17,25},{25,1},{2,10},{10... | collective-permute-start | bytes 245768 | tf_op jit(solution)/shard_map/ppermute | solution.py:15
  10.3 5.5 %collective-permute-start.2 = (f32[2,8,2,640]{3,2,1,0:T(2,128)S(1)}, f32[2,8,2,640]{3,2,1,0:T(2,128)S(1)}, u32[]{:S(2)}, u32[]{:S(2)}) collective-permute-start(f32[2,8,2,640]{3,2,1,0:T(2,128)S(1)} %get-tuple-element.68), channel_id=1, source_target_pairs={{0,1},{1,2},{2,3},{3,4},{4,5},{5,6},{6,7},{8,9},{9,10},{10,11},{11... | collective-permute-start | bytes 245768 | tf_op jit(solution)/shard_map/ppermute | solution.py:15
  13.8 6.3 %collective-permute-start.3 = (f32[2,8,2,640]{3,2,1,0:T(2,128)S(1)}, f32[2,8,2,640]{3,2,1,0:T(2,128)S(1)}, u32[]{:S(2)}, u32[]{:S(2)}) collective-permute-start(f32[2,8,2,640]{3,2,1,0:T(2,128)S(1)} %get-tuple-element.69), channel_id=1, source_target_pairs={{1,0},{2,1},{3,2},{4,3},{5,4},{6,5},{7,6},{9,8},{10,9},{11,10},{12... | collective-permute-start | bytes 245768 | tf_op jit(solution)/shard_map/ppermute | solution.py:16
  15.1 5.8 %copy-start.2 = (f32[8,8,640]{2,1,0:T(8,128)S(1)}, f32[8,8,640]{2,1,0:T(8,128)}, u32[]{:S(2)}) copy-start(f32[8,8,640]{2,1,0:T(8,128)} %param.12) | copy-start | bytes 491524
  20.3 1.0 %copy-start.3 = (s32[8,8,640]{2,1,0:T(8,128)S(1)}, s32[8,8,640]{2,1,0:T(8,128)}, u32[]{:S(2)}) copy-start(s32[8,8,640]{2,1,0:T(8,128)} %param.13) | copy-start | bytes 491524
  27.8 37.5 %copy-start.5 = (s32[1,32]{1,0:T(1,128)S(1)}, s32[1,32]{1,0:T(1,128)}, u32[]{:S(2)}) copy-start(s32[1,32]{1,0:T(1,128)} %param.15) | copy-start | bytes 388
  28.5 40.0 %copy-start.6 = (s32[1,32]{1,0:T(1,128)S(1)}, s32[1,32]{1,0:T(1,128)}, u32[]{:S(2)}) copy-start(s32[1,32]{1,0:T(1,128)} %param.14) | copy-start | bytes 388
  62.7 4.1 %collective-permute-start.4 = (f32[13,32]{1,0:T(8,128)S(1)}, f32[13,32]{1,0:T(8,128)S(1)}, u32[]{:S(2)}, u32[]{:S(2)}) collective-permute-start(f32[13,32]{1,0:T(8,128)S(1)} %get-tuple-element.30), channel_id=1, source_target_pairs={{0,1},{1,0},{2,3},{3,2},{4,5},{5,4},{6,7},{7,6},{8,9},{9,8},{10,11... | collective-permute-start | bytes 5000 | tf_op jit(solution)/shard_map/ppermute | solution.py:135
  66.9 3.7 %collective-permute-start.5 = (f32[13,32]{1,0:T(8,128)S(1)}, f32[13,32]{1,0:T(8,128)S(1)}, u32[]{:S(2)}, u32[]{:S(2)}) collective-permute-start(f32[13,32]{1,0:T(8,128)S(1)} %add.170), channel_id=1, source_target_pairs={{0,2},{1,3},{2,0},{3,1},{4,6},{5,7},{6,4},{7,5},{8,10},{9,11},{10,... | collective-permute-start | bytes 5000 | tf_op jit(solution)/shard_map/ppermute | solution.py:135
  70.5 4.5 %collective-permute-start.6 = (f32[13,32]{1,0:T(8,128)S(1)}, f32[13,32]{1,0:T(8,128)S(1)}, u32[]{:S(2)}, u32[]{:S(2)}) collective-permute-start(f32[13,32]{1,0:T(8,128)S(1)} %add.171), channel_id=1, source_target_pairs={{0,4},{1,5},{2,6},{3,7},{4,0},{5,1},{6,2},{7,3},{8,12},{9,13},{10,... | collective-permute-start | bytes 5000 | tf_op jit(solution)/shard_map/ppermute | solution.py:135
